TPU v7x, 32 devices: a whole 2x2x4 slice. The times are simulated.
32 devices in a mesh: dp: 8 (over z, y), tensor: 4 (over x, core).
Axes of the slice: x: 2, y: 2, z: 4, core: 2. Of those that a mesh axis runs over, the one named last changes fastest.
Arguments:
- tokens: bfloat16 [16384, 768], P(('dp', 'tensor')), may hold values from -6 to 6
- seq_lengths: int32 [8], replicated, may hold values from 1 to 2048, 10240 in all
- positions: int32 [8, 2048], P('dp'), may hold values from 0 to 2047, each once within a row
- w_query: bfloat16 [768, 768], P('dp', 'tensor'), may hold values from -0.21875 to 0.21875
- w_key: bfloat16 [768, 768], P('dp', 'tensor'), may hold values from -0.21875 to 0.21875
- w_value: bfloat16 [768, 768], P('dp', 'tensor'), may hold values from -0.21875 to 0.21875
- w_out: bfloat16 [768, 768], P('tensor', 'dp'), may hold values from -6 to 6
- w_up: bfloat16 [768, 3072], P('dp', 'tensor'), may hold values from -0.21875 to 0.21875
- w_down: bfloat16 [3072, 768], P('tensor', 'dp'), may hold values from -0.109375 to 0.109375
- b_query: bfloat16 [768], P('tensor'), may hold values from -3 to 3
- b_value: bfloat16 [768], P('tensor'), may hold values from -0.1796875 to 0.1796875
- b_out: bfloat16 [768], replicated, may hold values from -1.796875 to 1.796875
- b_up: bfloat16 [3072], P('tensor'), may hold values from -1.796875 to 1.796875
- b_down: bfloat16 [768], replicated, may hold values from -1.796875 to 1.796875
- gain_attn: bfloat16 [768], replicated, may hold values from 0.5 to 1.5
- shift_attn: bfloat16 [768], replicated, may hold values from -1.796875 to 1.796875
- gain_ffn: bfloat16 [768], replicated, may hold values from 0.5 to 1.5
- shift_ffn: bfloat16 [768], replicated, may hold values from -1.796875 to 1.796875
- out_grad: bfloat16 [16384, 768], P(('dp', 'tensor')), may hold values from -6 to 6
Outputs:
- layer_out: bfloat16 [16384, 768], P(('dp', 'tensor'))
- input_grad: bfloat16 [16384, 768], P(('dp', 'tensor'))
- grad_w_query: float32 [768, 768], P('dp', 'tensor')
- grad_w_key: float32 [768, 768], P('dp', 'tensor')
- grad_w_value: float32 [768, 768], P('dp', 'tensor')
- grad_w_out: float32 [768, 768], P('tensor', 'dp')
- grad_w_up: float32 [768, 3072], P('dp', 'tensor')
- grad_w_down: float32 [3072, 768], P('tensor', 'dp')
- grad_b_query: float32 [768], P('tensor')
- grad_b_value: float32 [768], P('tensor')
- grad_b_out: float32 [768], replicated
- grad_b_up: float32 [3072], P('tensor')
- grad_b_down: float32 [768], replicated
- grad_gain_attn: float32 [768], replicated
- grad_shift_attn: float32 [768], replicated
- grad_gain_ffn: float32 [768], replicated
- grad_shift_ffn: float32 [768], replicated
- rms: float32 [3], replicated
Inputs may be any that keep to these rules, and one draw needn't show every extreme that they name: `seq_lengths`: one length for each slot; the longest equals 2048. `positions`: each row is a permutation of 0 to 2047.
All inputs are finite; a program needn't handle non-finite values.
Results may differ from a plain program's by a relative error of at most 0.019.
Values may be sent and summed in bfloat16 or wider, within the bound.
No kernel may reach another device: no remote copies, remote signals or barrier semaphores. Data moves between devices by JAX's collectives and lax.ppermute only.
A program may use at most 128 MiB of HBM per device.

v0:
```python
import jax
import jax.numpy as jnp
from jax import lax
from jax.sharding import PartitionSpec as P

D = 768
HEAD_DIM = 64
EPSILON = 1e-12
MASKED = -1e30


def norm_rows(rows, scale_vec, shift_vec):
    average = jnp.mean(rows, axis=-1, keepdims=True)
    centred = rows - average
    variance = jnp.mean(centred * centred, axis=-1, keepdims=True)
    return centred * lax.rsqrt(variance + EPSILON) * scale_vec + shift_vec


def gelu_exact(values_in):
    return jax.nn.gelu(values_in, approximate=False)


def product(left, right):
    return jnp.dot(left, right, preferred_element_type=jnp.float32)


def product_tn(left, right):
    return lax.dot_general(
        left, right, (((0,), (0,)), ((), ())), preferred_element_type=jnp.float32
    )


def product_nt(left, right):
    return lax.dot_general(
        left, right, (((1,), (1,)), ((), ())), preferred_element_type=jnp.float32
    )


def block_scores(query_block, keys_all, key_valid, scale_value):
    scores = (
        jnp.einsum("qhd,khd->hqk", query_block, keys_all, preferred_element_type=jnp.float32)
        * scale_value
    )
    return jnp.where(key_valid[None, None, :], scores, MASKED)


def attention_forward(queries, keys_all, values_all, key_valid, block_rows):
    seq_len, heads_local, head_size = queries.shape
    scale_value = head_size ** (-0.5)

    def one_block(query_block):
        scores = block_scores(query_block, keys_all, key_valid, scale_value)
        top_score = jnp.max(scores, axis=-1, keepdims=True)
        expon = jnp.exp(scores - top_score)
        row_total = jnp.sum(expon, axis=-1, keepdims=True)
        probs = (expon / row_total).astype(jnp.bfloat16)
        attended = jnp.einsum("hqk,khd->qhd", probs, values_all, preferred_element_type=jnp.float32)
        return (attended, (top_score + jnp.log(row_total))[..., 0])

    shaped = queries.reshape(seq_len // block_rows, block_rows, heads_local, head_size)
    attended, log_total = lax.map(one_block, shaped)
    return (attended.reshape(seq_len, heads_local * head_size).astype(jnp.bfloat16), log_total)


def attention_backward(
    queries, keys_all, values_all, key_valid, log_total, grad_attended, block_rows
):
    seq_len, heads_local, head_size = queries.shape
    scale_value = head_size ** (-0.5)

    def one_block(carry, block_index):
        grad_keys, grad_values = carry
        start = block_index * block_rows
        query_block = lax.dynamic_slice_in_dim(queries, start, block_rows, 0)
        grad_block = lax.dynamic_slice_in_dim(grad_attended, start, block_rows, 0)
        scores = block_scores(query_block, keys_all, key_valid, scale_value)
        probs = jnp.exp(scores - log_total[block_index][..., None])
        grad_probs = jnp.einsum(
            "qhd,khd->hqk", grad_block, values_all, preferred_element_type=jnp.float32
        )
        row_delta = jnp.sum(probs * grad_probs, axis=-1, keepdims=True)
        grad_scores = (probs * (grad_probs - row_delta)).astype(jnp.bfloat16)
        grad_query = (
            jnp.einsum("hqk,khd->qhd", grad_scores, keys_all, preferred_element_type=jnp.float32)
            * scale_value
        )
        grad_keys = (
            grad_keys
            + jnp.einsum(
                "hqk,qhd->khd", grad_scores, query_block, preferred_element_type=jnp.float32
            )
            * scale_value
        )
        grad_values = grad_values + jnp.einsum(
            "hqk,qhd->khd",
            probs.astype(jnp.bfloat16),
            grad_block,
            preferred_element_type=jnp.float32,
        )
        return ((grad_keys, grad_values), grad_query)

    initial = (jnp.zeros(keys_all.shape, jnp.float32), jnp.zeros(values_all.shape, jnp.float32))
    (grad_keys, grad_values), grad_queries = lax.scan(
        one_block, initial, jnp.arange(seq_len // block_rows)
    )
    width_local = heads_local * head_size
    return (
        grad_queries.reshape(seq_len, width_local).astype(jnp.bfloat16),
        grad_keys.reshape(seq_len, width_local).astype(jnp.bfloat16),
        grad_values.reshape(seq_len, width_local).astype(jnp.bfloat16),
    )


def body(
    tokens,
    seq_lengths,
    positions,
    w_query,
    w_key,
    w_value,
    w_out,
    w_up,
    w_down,
    b_query,
    b_value,
    b_out,
    b_up,
    b_down,
    gain_attn,
    shift_attn,
    gain_ffn,
    shift_ffn,
    out_grad,
):
    group = lax.axis_index("dp")
    member = lax.axis_index("tensor")
    tensor_count = lax.axis_size("tensor")
    tok_rows = tokens.shape[0]
    seq_len = tok_rows * tensor_count
    block_rows = min(512, seq_len)
    length = lax.dynamic_index_in_dim(seq_lengths, group, 0, keepdims=False)
    key_valid = positions[0] < length
    row_valid = lax.dynamic_slice_in_dim(key_valid, member * tok_rows, tok_rows, 0)
    query_mat, key_mat, value_mat, out_mat, up_mat, down_mat = (
        lax.all_gather(w_query, "dp", axis=0, tiled=True),
        lax.all_gather(w_key, "dp", axis=0, tiled=True),
        lax.all_gather(w_value, "dp", axis=0, tiled=True),
        lax.all_gather(w_out, "dp", axis=1, tiled=True),
        lax.all_gather(w_up, "dp", axis=0, tiled=True),
        lax.all_gather(w_down, "dp", axis=1, tiled=True),
    )
    width_local = query_mat.shape[1]
    heads_local = width_local // HEAD_DIM
    up_local = b_up.shape[0]
    shape_heads = (seq_len, heads_local, HEAD_DIM)
    inputs_own = tokens.astype(jnp.float32)
    gathered = lax.all_gather(tokens, "tensor", axis=0, tiled=True)
    queries = (
        (product(gathered, query_mat) + b_query.astype(jnp.float32))
        .astype(jnp.bfloat16)
        .reshape(shape_heads)
    )
    keys_all = product(gathered, key_mat).astype(jnp.bfloat16).reshape(shape_heads)
    values_all = (
        (product(gathered, value_mat) + b_value.astype(jnp.float32))
        .astype(jnp.bfloat16)
        .reshape(shape_heads)
    )
    attended, log_total = attention_forward(queries, keys_all, values_all, key_valid, block_rows)
    attn_out = lax.psum_scatter(
        product(attended, out_mat), "tensor", scatter_dimension=0, tiled=True
    ) + b_out.astype(jnp.float32)
    normed, pull_one = jax.vjp(
        norm_rows,
        inputs_own + attn_out,
        gain_attn.astype(jnp.float32),
        shift_attn.astype(jnp.float32),
    )
    normed_low = normed.astype(jnp.bfloat16)
    normed_all = lax.all_gather(normed_low, "tensor", axis=0, tiled=True)
    hidden_pre = product(normed_all, up_mat) + b_up.astype(jnp.float32)
    hidden_act, pull_gelu = jax.vjp(gelu_exact, hidden_pre)
    hidden = hidden_act.astype(jnp.bfloat16)
    ffn_part = lax.psum_scatter(
        product(hidden, down_mat), "tensor", scatter_dimension=0, tiled=True
    )
    ffn_out = ffn_part + b_down.astype(jnp.float32)
    layer_out, pull_two = jax.vjp(
        norm_rows, normed + ffn_out, gain_ffn.astype(jnp.float32), shift_ffn.astype(jnp.float32)
    )
    grad_two, grad_gain_ffn, grad_shift_ffn = pull_two(out_grad.astype(jnp.float32))
    grad_ffn_low = grad_two.astype(jnp.bfloat16)
    grad_bias_down = jnp.sum(grad_ffn_low, axis=0, dtype=jnp.float32)
    grad_ffn_all = lax.all_gather(grad_ffn_low, "tensor", axis=0, tiled=True)
    grad_hidden = product_nt(grad_ffn_all, down_mat)
    grad_down = product_tn(hidden, grad_ffn_all)
    grad_pre = pull_gelu(grad_hidden)[0].astype(jnp.bfloat16)
    grad_up = product_tn(normed_all, grad_pre)
    bias_up_sum = jnp.sum(grad_pre, axis=0, dtype=jnp.float32)
    grad_bias_up = lax.dynamic_update_slice_in_dim(
        jnp.zeros((up_local * tensor_count,), jnp.float32), bias_up_sum, member * up_local, 0
    )
    grad_normed_ffn = lax.psum_scatter(
        product_nt(grad_pre, up_mat), "tensor", scatter_dimension=0, tiled=True
    )
    grad_one, grad_gain_attn, grad_shift_attn = pull_one(grad_two + grad_normed_ffn)
    grad_attn_low = grad_one.astype(jnp.bfloat16)
    grad_bias_out = jnp.sum(grad_attn_low, axis=0, dtype=jnp.float32)
    grad_attn_all = lax.all_gather(grad_attn_low, "tensor", axis=0, tiled=True)
    grad_out = product_tn(attended, grad_attn_all)
    grad_attended = product_nt(grad_attn_all, out_mat).astype(jnp.bfloat16).reshape(shape_heads)
    grad_q_low, grad_k_low, grad_v_low = attention_backward(
        queries, keys_all, values_all, key_valid, log_total, grad_attended, block_rows
    )
    grad_query = product_tn(gathered, grad_q_low)
    grad_key = product_tn(gathered, grad_k_low)
    grad_value = product_tn(gathered, grad_v_low)
    part_q = product_nt(grad_q_low, query_mat)
    part_k = product_nt(grad_k_low, key_mat)
    part_v = product_nt(grad_v_low, value_mat)
    grad_inputs = lax.psum_scatter(
        (part_q + part_k + part_v).astype(jnp.bfloat16), "tensor", scatter_dimension=0, tiled=True
    ).astype(jnp.float32)
    input_grad = (grad_one + grad_inputs).astype(jnp.bfloat16)
    summed_w = (
        lax.psum_scatter(grad_query, "dp", scatter_dimension=0, tiled=True),
        lax.psum_scatter(grad_key, "dp", scatter_dimension=0, tiled=True),
        lax.psum_scatter(grad_value, "dp", scatter_dimension=0, tiled=True),
        lax.psum_scatter(grad_out, "dp", scatter_dimension=1, tiled=True),
        lax.psum_scatter(grad_up, "dp", scatter_dimension=0, tiled=True),
        lax.psum_scatter(grad_down, "dp", scatter_dimension=1, tiled=True),
    )
    full_width = width_local * tensor_count
    bias_query_full = lax.dynamic_update_slice_in_dim(
        jnp.zeros((full_width,), jnp.float32),
        jnp.sum(grad_q_low, axis=0, dtype=jnp.float32),
        member * width_local,
        0,
    )
    bias_value_full = lax.dynamic_update_slice_in_dim(
        jnp.zeros((full_width,), jnp.float32),
        jnp.sum(grad_v_low, axis=0, dtype=jnp.float32),
        member * width_local,
        0,
    )
    row_mask = row_valid[:, None]
    squares = jnp.stack(
        [
            jnp.sum(jnp.where(row_mask, field * field, 0.0))
            for field in (inputs_own, attn_out, ffn_out)
        ]
    )
    summed = lax.psum(
        (
            bias_query_full,
            bias_value_full,
            grad_bias_out,
            grad_bias_up,
            grad_bias_down,
            grad_gain_attn,
            grad_shift_attn,
            grad_gain_ffn,
            grad_shift_ffn,
            squares,
        ),
        ("dp", "tensor"),
    )
    count = jnp.sum(seq_lengths).astype(jnp.float32) * D
    rms = jnp.sqrt(summed[9] / count)
    grad_b_query = lax.dynamic_slice_in_dim(summed[0], member * width_local, width_local, 0)
    grad_b_value = lax.dynamic_slice_in_dim(summed[1], member * width_local, width_local, 0)
    grad_b_up = lax.dynamic_slice_in_dim(summed[3], member * up_local, up_local, 0)
    return (
        layer_out.astype(jnp.bfloat16),
        input_grad,
        summed_w[0],
        summed_w[1],
        summed_w[2],
        summed_w[3],
        summed_w[4],
        summed_w[5],
        grad_b_query,
        grad_b_value,
        summed[2],
        grad_b_up,
        summed[4],
        summed[5],
        summed[6],
        summed[7],
        summed[8],
        rms,
    )


def solution(mesh):
    in_specs = (
        P(("dp", "tensor"), None),
        P(),
        P("dp", None),
        P("dp", "tensor"),
        P("dp", "tensor"),
        P("dp", "tensor"),
        P("tensor", "dp"),
        P("dp", "tensor"),
        P("tensor", "dp"),
        P("tensor"),
        P("tensor"),
        P(),
        P("tensor"),
        P(),
        P(),
        P(),
        P(),
        P(),
        P(("dp", "tensor"), None),
    )
    out_specs = (
        P(("dp", "tensor"), None),
        P(("dp", "tensor"), None),
        P("dp", "tensor"),
        P("dp", "tensor"),
        P("dp", "tensor"),
        P("tensor", "dp"),
        P("dp", "tensor"),
        P("tensor", "dp"),
        P("tensor"),
        P("tensor"),
        P(),
        P("tensor"),
        P(),
        P(),
        P(),
        P(),
        P(),
        P(),
    )
    return jax.shard_map(body, mesh=mesh, in_specs=in_specs, out_specs=out_specs, check_vma=False)
```

profile of v0, /device:TPU:0, one launch (start us, length us, event | category | flops | bytes accessed | tf_op | source)
XLA Modules:
  0.0 1126.0 jit_solution(8384975540335795945)
XLA Ops:
  12.3 32.9 %all_gather.34 = bf16[192,768]{0,1:T(8,128)(2,1)S(1)} all-gather(bf16[192,96]{0,1:T(8,128)(2,1)S(1)} %copy.49), channel_id=1, replica_groups=mesh['dp'=8,'tensor'=4] {'dp'}, dimensions={1}, use_global_device_ids=true | all-gather | bytes 331776 | tf_op jit(solution)/shard_map/all_gather | solution.py:148
  45.2 31.3 %all_gather.31 = bf16[768,192]{1,0:T(8,128)(2,1)S(1)} all-gather(bf16[96,192]{1,0:T(8,128)(2,1)} %param.26), channel_id=1, replica_groups=mesh['dp'=8,'tensor'=4] {'dp'}, dimensions={0}, use_global_device_ids=true | all-gather | bytes 331776 | tf_op jit(solution)/shard_map/all_gather | solution.py:145
  76.6 31.5 %all_gather.32 = bf16[768,192]{1,0:T(8,128)(2,1)S(1)} all-gather(bf16[96,192]{1,0:T(8,128)(2,1)} %param.27), channel_id=1, replica_groups=mesh['dp'=8,'tensor'=4] {'dp'}, dimensions={0}, use_global_device_ids=true | all-gather | bytes 331776 | tf_op jit(solution)/shard_map/all_gather | solution.py:146
  108.1 33.2 %all_gather.33 = bf16[768,192]{1,0:T(8,128)(2,1)} all-gather(bf16[96,192]{1,0:T(8,128)(2,1)} %param.28), channel_id=1, replica_groups=mesh['dp'=8,'tensor'=4] {'dp'}, dimensions={0}, use_global_device_ids=true | all-gather | bytes 331776 | tf_op jit(solution)/shard_map/all_gather | solution.py:147
  143.2 3.1 fusion.43
  147.3 3.2 convolution_convert_fusion.1
  151.8 36.4 %while.27 = (s32[]{:T(128)}, bf16[4,512,3,64]{1,3,2,0:T(8,128)(2,1)S(1)}, f32[4,3,512]{2,1,0:T(4,128)}, pred[2048]{0:T(1024)(128)(4,1)S(1)}, bf16[4,512,3,64]{1,...) while((s32[]{:T(128)}, ...), condition=%wide.region_3.4_spmd, body=%wide.region_0.3_spmd.sunk | while | flops 843053568 | bytes 39972968 | solution.py:61
  153.8 2.8 fusion.131
  156.6 3.7 fusion.132
  162.9 2.8 fusion.131
  165.7 3.7 fusion.132
  172.0 2.8 fusion.131
  174.8 3.7 fusion.132
  181.1 2.8 fusion.131
  183.9 3.7 fusion.132
  189.9 3.7 fusion.60
  195.0 58.1 %reduce-scatter.19.cloned.1.call-done = f32[512,768]{1,0:T(8,128)} async-done(((f32[2048,768]{1,0:T(8,128)}), f32[512,768]{1,0:T(8,128)}) %reduce-scatter.19.cloned.1.call-update) | async-done | bytes 1572880 | tf_op jit(solution)/shard_map/reduce_scatter | solution.py:170
  259.2 26.4 %all-gather.9.cloned.1.call-done = bf16[2048,768]{1,0:T(8,128)(2,1)} async-done(((bf16[512,768]{1,0:T(8,128)(2,1)}), bf16[2048,768]{1,0:T(8,128)(2,1)}) %all-gather.9.cloned.1.call-update) | async-done | bytes 3145744 | tf_op jit(solution)/shard_map/all_gather | solution.py:180
  285.6 18.9 %multiply_convert_fusion.1 = (bf16[2048,768]{1,0:T(8,128)(2,1)}, f32[2048,768]{1,0:T(8,128)}, f32[2048,768]{1,0:T(8,128)}) fusion(f32[768]{0:T(1024)} %convert_element_type.139, bf16[2048,768]{1,0:T(8,128)(2,1)} %all-gather.9.cloned.1.call-done, bf16[768,768]{1,0:T(8,128)(2,1)} %all-gather.11.cloned.1.call-done), kind=kOutput, calls=%fused_computation.47 | convolution fusion | flops 2519728128 | bytes 20057088 | tf_op jit(solution)/shard_map/dot_general | solution.py:24
  304.5 24.9 %all-gather.13.cloned.1.call-done = bf16[768,768]{0,1:T(8,128)(2,1)} async-done(((bf16[768,96]{0,1:T(8,128)(2,1)}), bf16[768,768]{0,1:T(8,128)(2,1)}) %all-gather.13.cloned.1.call-update) | async-done | bytes 1179664 | tf_op jit(solution)/shard_map/all_gather | solution.py:150
  329.4 7.5 fusion.61
  342.1 51.7 %reduce-scatter.21.cloned.1.call-done = f32[512,768]{1,0:T(8,128)} async-done(((f32[2048,768]{1,0:T(8,128)}), f32[512,768]{1,0:T(8,128)}) %reduce-scatter.21.cloned.1.call-update) | async-done | bytes 1572880 | tf_op jit(solution)/shard_map/reduce_scatter | solution.py:184
  393.8 4.2 fusion.49
  404.5 28.2 %all-gather.15.cloned.1.call-done = bf16[2048,768]{1,0:T(8,128)(2,1)} async-done(((bf16[512,768]{1,0:T(8,128)(2,1)}), bf16[2048,768]{1,0:T(8,128)(2,1)}) %all-gather.15.cloned.1.call-update) | async-done | bytes 3145744 | tf_op jit(solution)/shard_map/all_gather | solution.py:194
  432.7 11.1 convert_reduce_fusion
  445.4 4.6 fusion.62
  450.1 58.3 %reduce-scatter.23.cloned.1.call-done = f32[512,768]{1,0:T(8,128)} async-done(((f32[2048,768]{1,0:T(8,128)}), f32[512,768]{1,0:T(8,128)}) %reduce-scatter.23.cloned.1.call-update) | async-done | bytes 1572880 | tf_op jit(solution)/shard_map/reduce_scatter | solution.py:203
  508.4 3.3 multiply_reduce_fusion.1
  516.1 28.4 %all-gather.17.cloned.1.call-done = bf16[2048,768]{1,0:T(8,128)(2,1)} async-done(((bf16[512,768]{1,0:T(8,128)(2,1)}), bf16[2048,768]{1,0:T(8,128)(2,1)}) %all-gather.17.cloned.1.call-update) | async-done | bytes 3145744 | tf_op jit(solution)/shard_map/all_gather | solution.py:209
  544.6 4.0 convolution_convert_fusion
  549.5 119.3 %while.28 = (s32[]{:T(128)}, f32[2048,3,64]{0,2,1:T(8,128)S(1)}, f32[2048,3,64]{0,2,1:T(8,128)}, bf16[4,512,3,64]{1,3,2,0:T(8,128)(2,1)}, s32[4]{0:T(128)S(1)}, ...) while((s32[]{:T(128)}, f32[2048,3,64]{0,2,1:T(8,128)S(1)}, ...), condition=%wide.region_17.18_spmd.clone, body=%wide.region_15.17_spmd.clone.sunk | while | flops 2062514688 | bytes 129417528 | solution.py:103
  553.4 2.8 fusion.142
  556.1 4.9 fusion.144
  561.0 4.8 multiply_reduce_fusion.6
  565.9 5.0 multiply_convert_fusion.3
  570.9 5.6 fusion.145
  582.8 2.8 fusion.142
  585.5 5.5 fusion.144
  591.0 4.8 multiply_reduce_fusion.6
  595.9 5.0 multiply_convert_fusion.3
  600.9 5.6 fusion.145
  612.7 2.8 fusion.142
  615.5 5.5 fusion.144
  621.0 4.8 multiply_reduce_fusion.6
  625.9 5.0 multiply_convert_fusion.3
  630.8 5.6 fusion.145
  642.7 2.8 fusion.142
  645.5 5.5 fusion.144
  651.0 4.8 multiply_reduce_fusion.6
  655.9 5.0 multiply_convert_fusion.3
  660.8 5.6 fusion.145
  668.9 4.5 convolution_bitcast_fusion
  678.3 2.8 add_convert_fusion
  681.2 7.0 fusion.65
  688.2 6.9 fusion.66
  695.2 3.5 convolution_bitcast_fusion.3
  705.4 3.7 convolution_bitcast_fusion.1
  715.7 40.9 %all-reduce = (f32[768]{0:T(1024)S(1)}, f32[768]{0:T(1024)S(1)}, f32[768]{0:T(1024)}, f32[3072]{0:T(1024)S(1)}, f32[768]{0:T(1024)}, /*index=5*/f32[768]{0:T(102...) all-reduce(f32[768]{0:T(1024)S(1)} %dynamic_update_slice.20, ...), channel_id=1, replica_groups=mesh['dp'=8,'tensor'=4] {'dp','tensor'}, use_global_device_ids=true, to_apply=%region_26.27 | all-reduce | flops 9219 | bytes 73752 | tf_op jit(solution)/shard_map/psum | solution.py:253
  760.7 14.7 %reduce-scatter.25.cloned.1.call-done = bf16[512,768]{1,0:T(8,128)(2,1)} async-done(((bf16[2048,768]{1,0:T(8,128)(2,1)}), bf16[512,768]{1,0:T(8,128)(2,1)}) %reduce-scatter.25.cloned.1.call-update) | async-done | bytes 786448 | tf_op jit(solution)/shard_map/reduce_scatter | solution.py:221
  777.6 71.3 %reduce-scatter.27.cloned.1.call-done = f32[96,768]{1,0:T(8,128)} async-done(((f32[768,768]{1,0:T(8,128)}), f32[96,768]{1,0:T(8,128)}) %reduce-scatter.27.cloned.1.call-update) | async-done | bytes 294928 | tf_op jit(solution)/shard_map/reduce_scatter | solution.py:230
  849.0 72.3 %reduce-scatter.29.cloned.1.call-done = f32[768,96]{0,1:T(8,128)} async-done(((f32[768,768]{0,1:T(8,128)}), f32[768,96]{0,1:T(8,128)}) %reduce-scatter.29.cloned.1.call-update) | async-done | bytes 294928 | tf_op jit(solution)/shard_map/reduce_scatter | solution.py:231
  921.3 65.9 %reduce-scatter.31.cloned.1.call-done = f32[96,192]{1,0:T(8,128)} async-done(((f32[768,192]{1,0:T(8,128)}), f32[96,192]{1,0:T(8,128)}) %reduce-scatter.31.cloned.1.call-update) | async-done | bytes 73744
  987.2 65.3 %reduce-scatter.33.cloned.1.call-done = f32[96,192]{1,0:T(8,128)} async-done(((f32[768,192]{1,0:T(8,128)}), f32[96,192]{1,0:T(8,128)}) %reduce-scatter.33.cloned.1.call-update) | async-done | bytes 73744
  1052.6 65.9 %reduce-scatter.35.cloned.1.call-done = f32[96,192]{1,0:T(8,128)} async-done(((f32[768,192]{1,0:T(8,128)}), f32[96,192]{1,0:T(8,128)}) %reduce-scatter.35.cloned.1.call-update) | async-done | bytes 73744
  (201 shorter events, 85.0 us)
Async XLA Ops:
  8.0 135.2 %all-gather.7.cloned.1.call-start = ((), (), s32[]{:S(2)}) async-start(), calls=%async_computation.10 | async-start | bytes 3932160 | tf_op jit(solution)/shard_map/all_gather | solution.py:157
  8.8 244.3 %reduce-scatter.19.cloned.1.call-start = ((), (), s32[]{:S(2)}) async-start(), calls=%async_computation.11 | async-start | bytes 7864320 | tf_op jit(solution)/shard_map/reduce_scatter | solution.py:170
  76.6 70.3 %copy-start.11 = (bf16[768,192]{1,0:T(8,128)(2,1)}, bf16[768,192]{1,0:T(8,128)(2,1)S(1)}, u32[]{:S(2)}) copy-start(bf16[768,192]{1,0:T(8,128)(2,1)S(1)} %all_gather.31) | copy-start | bytes 884740
  108.0 39.3 %copy-start.8 = (bf16[768,192]{1,0:T(8,128)(2,1)}, bf16[768,192]{1,0:T(8,128)(2,1)S(1)}, u32[]{:S(2)}) copy-start(bf16[768,192]{1,0:T(8,128)(2,1)S(1)} %all_gather.32) | copy-start | bytes 884740
  146.2 0.9 copy-start.5
  147.1 3.4 copy-start.1
  147.1 3.4 copy-start.13
  189.0 0.9 copy-start.7
  193.7 0.7 copy-start.30
  193.7 0.7 copy-start.31
  193.7 0.7 copy-start.32
  193.7 65.5 %all-gather.11.cloned.1.call-start = ((), (), s32[]{:S(2)}) async-start(), calls=%async_computation.13 | async-start | bytes 1327104 | tf_op jit(solution)/shard_map/all_gather | solution.py:149
  194.3 91.3 %all-gather.9.cloned.1.call-start = ((), (), s32[]{:S(2)}) async-start(), calls=%async_computation.12 | async-start | bytes 3932160 | tf_op jit(solution)/shard_map/all_gather | solution.py:180
  194.4 60.6 %copy-start.17 = (f32[768]{0:T(1024)}, f32[768]{0:T(1024)S(1)}, u32[]{:S(2)}) copy-start(f32[768]{0:T(1024)S(1)} %convert_element_type.135) | copy-start | bytes 9220
  253.1 2.8 copy-start.15
  255.3 0.6 copy-start.18
  257.1 72.4 %all-gather.13.cloned.1.call-start = ((), (), s32[]{:S(2)}) async-start(), calls=%async_computation.14 | async-start | bytes 1327104 | tf_op jit(solution)/shard_map/all_gather | solution.py:150
  257.7 136.1 %reduce-scatter.21.cloned.1.call-start = ((), (), s32[]{:S(2)}) async-start(), calls=%async_computation.15 | async-start | bytes 7864320 | tf_op jit(solution)/shard_map/reduce_scatter | solution.py:184
  337.0 95.7 %all-gather.15.cloned.1.call-start = ((), (), s32[]{:S(2)}) async-start(), calls=%async_computation.16 | async-start | bytes 3932160 | tf_op jit(solution)/shard_map/all_gather | solution.py:194
  393.8 4.5 copy-start.10
  393.8 4.5 copy-start.16
  398.0 1.6 copy-start.26
  401.1 1.2 copy-start.4
  401.1 2.8 copy-start.19
  404.0 104.4 %reduce-scatter.23.cloned.1.call-start = ((), (), s32[]{:S(2)}) async-start(), calls=%async_computation.17 | async-start | bytes 7864320 | tf_op jit(solution)/shard_map/reduce_scatter | solution.py:203
  432.7 12.7 %copy-start.33 = (bf16[768,768]{1,0:T(8,128)(2,1)S(1)}, bf16[768,768]{1,0:T(8,128)(2,1)}, u32[]{:S(2)}) copy-start(bf16[768,768]{1,0:T(8,128)(2,1)} %all-gather.11.cloned.1.call-done) | copy-start | bytes 3538948
  443.8 1.7 copy-start.35
  450.0 94.5 %all-gather.17.cloned.1.call-start = ((), (), s32[]{:S(2)}) async-start(), calls=%async_computation.18 | async-start | bytes 3932160 | tf_op jit(solution)/shard_map/all_gather | solution.py:209
  513.0 1.2 copy-start.2
  513.0 2.8 copy-start.20
  515.9 243.2 %reduce-scatter.37.cloned.1.call-start = ((), (), s32[]{:S(2)}) async-start(), calls=%async_computation.25 | async-start | bytes 884736
  570.9 5.6 copy-start
  600.8 5.6 copy-start
  630.8 5.6 copy-start
  660.8 5.6 copy-start
  668.9 4.8 copy-start.9
  673.4 102.0 %reduce-scatter.25.cloned.1.call-start = ((), (), s32[]{:S(2)}) async-start(), calls=%async_computation.19 | async-start | bytes 3932160 | tf_op jit(solution)/shard_map/reduce_scatter | solution.py:221
  673.7 2.7 copy-start.6
  674.8 2.5 copy-start.12
  677.2 1.1 copy-start.14
  681.1 167.8 %reduce-scatter.27.cloned.1.call-start = ((), (), s32[]{:S(2)}) async-start(), calls=%async_computation.20 | async-start | bytes 2654208 | tf_op jit(solution)/shard_map/reduce_scatter | solution.py:230
  688.2 233.1 %reduce-scatter.29.cloned.1.call-start = ((), (), s32[]{:S(2)}) async-start(), calls=%async_computation.21 | async-start | bytes 2654208 | tf_op jit(solution)/shard_map/reduce_scatter | solution.py:231
  695.2 292.1 %reduce-scatter.31.cloned.1.call-start = ((), (), s32[]{:S(2)}) async-start(), calls=%async_computation.22 | async-start | bytes 884736
  701.0 351.5 %reduce-scatter.33.cloned.1.call-start = ((), (), s32[]{:S(2)}) async-start(), calls=%async_computation.23 | async-start | bytes 884736
  705.0 6.3 copy-start.34
  705.0 9.6 copy-start.29
  705.0 10.7 copy-start.22
  705.0 10.6 copy-start.23
  705.0 10.6 copy-start.24
  705.0 10.6 copy-start.25
  705.0 10.6 copy-start.27
  705.0 10.6 copy-start.28
  705.1 70.3 %copy-start.3 = (f32[512,768]{1,0:T(8,128)S(1)}, f32[512,768]{1,0:T(8,128)}, u32[]{:S(2)}) copy-start(f32[512,768]{1,0:T(8,128)} %copy-done.2) | copy-start | bytes 4718596
  705.1 70.3 %copy-start.21 = (f32[512]{0:T(512)S(1)}, f32[512]{0:T(512)}, u32[]{:S(2)}) copy-start(f32[512]{0:T(512)} %copy-done.20) | copy-start | bytes 6148
  705.1 413.3 %reduce-scatter.35.cloned.1.call-start = ((), (), s32[]{:S(2)}) async-start(), calls=%async_computation.24 | async-start | bytes 884736
Sparse Core Ops, SparseCore 0:
  10.4 31.2 all-gather.6
  193.8 59.2 reduce-scatter.18
  404.1 28.5 all-gather.14
  516.0 28.5 all-gather.16
Sparse Core Ops, SparseCore 1:
  196.6 42.3 all-gather.10
  257.2 28.4 all-gather.8
  287.9 41.5 all-gather.12
  337.0 56.7 reduce-scatter.20
  450.1 58.2 reduce-scatter.22
  673.5 62.5 reduce-scatter.36
  738.5 36.8 reduce-scatter.24
  779.7 69.2 reduce-scatter.26
  853.3 67.9 reduce-scatter.28
  925.5 61.6 reduce-scatter.30
  991.0 61.5 reduce-scatter.32
  1056.8 61.5 reduce-scatter.34
where the time goes:
time: 1140 us; the launch traced here: 1130 us
  waiting for transfers between devices  634 us (56%)
  matrix products  197 us (17%)
  blocking collectives  170 us (15%)
  other arithmetic  68.6 us (6%)
  local copies, waits for them, and re-layouts  27.8 us (2%)
  between operations  17 us (1%)
    unnamed x20, waiting for transfers between devices  199 us
    reduce_scatter x1, waiting for transfers between devices, body(): lax.psum_scatter(grad_down, 'dp', scatter_dimension=1, tiled=True)  72.3 us
    reduce_scatter x1, waiting for transfers between devices, body(): lax.psum_scatter(grad_up, 'dp', scatter_dimension=0, tiled=True)  71.3 us
    reduce_scatter x1, waiting for transfers between devices, body(): lax.psum_scatter(product_nt(grad_pre, up_mat), 'tensor', scatter_dimensio...  58.3 us
    reduce_scatter x1, waiting for transfers between devices, body(): lax.psum_scatter(product(attended, out_mat), 'tensor', scatter_dimension=...  58.1 us
    reduce_scatter x1, waiting for transfers between devices, body(): lax.psum_scatter(product(hidden, down_mat), 'tensor', scatter_dimension=0...  51.7 us
    psum x1, blocking collectives, body(): lax.psum((bias_query_full, bias_value_full, grad_bias_out, grad_bias_up,...  40.9 us
    dot_general x6, matrix products, product(): return jnp.dot(left, right, preferred_element_type=jnp.float32)  37.6 us
  transfers between devices with their start and end apart: 16, of which 13 were waited for; matrix products, arithmetic and copies ran while one was open for 7% of the time, Pallas kernels for 0%

commit v1 on v0

--- a/solution.py
+++ b/solution.py
@@ -250,21 +250,20 @@
             for field in (inputs_own, attn_out, ffn_out)
         ]
     )
-    summed = lax.psum(
-        (
-            bias_query_full,
-            bias_value_full,
-            grad_bias_out,
-            grad_bias_up,
-            grad_bias_down,
-            grad_gain_attn,
-            grad_shift_attn,
-            grad_gain_ffn,
-            grad_shift_ffn,
-            squares,
-        ),
-        ("dp", "tensor"),
-    )
+    summed = (
+        bias_query_full,
+        bias_value_full,
+        grad_bias_out,
+        grad_bias_up,
+        grad_bias_down,
+        grad_gain_attn,
+        grad_shift_attn,
+        grad_gain_ffn,
+        grad_shift_ffn,
+        squares,
+    )
+    for over in ("tensor", "dp"):
+        summed = lax.psum(summed, over)
     count = jnp.sum(seq_lengths).astype(jnp.float32) * D
     rms = jnp.sqrt(summed[9] / count)
     grad_b_query = lax.dynamic_slice_in_dim(summed[0], member * width_local, width_local, 0)

time: 1140 us -> 1140 us (level)
    psum x1 -> x2, blocking collectives: 40.9 us -> 49.2 us  [body(): summed = lax.psum(summed, over)]
where the time goes in v1:
time: 1140 us; the launch traced here: 1130 us
  waiting for transfers between devices  625 us (55%)
  matrix products  197 us (17%)
  blocking collectives  178 us (16%)
  other arithmetic  68.6 us (6%)
  local copies, waits for them, and re-layouts  27.8 us (2%)
  between operations  17 us (1%)
    unnamed x20, waiting for transfers between devices  199 us
    reduce_scatter x1, waiting for transfers between devices, body(): lax.psum_scatter(grad_down, 'dp', scatter_dimension=1, tiled=True)  72.4 us
    reduce_scatter x1, waiting for transfers between devices, body(): lax.psum_scatter(grad_up, 'dp', scatter_dimension=0, tiled=True)  71.1 us
    reduce_scatter x1, waiting for transfers between devices, body(): lax.psum_scatter(product_nt(grad_pre, up_mat), 'tensor', scatter_dimensio...  58.3 us
    reduce_scatter x1, waiting for transfers between devices, body(): lax.psum_scatter(product(attended, out_mat), 'tensor', scatter_dimension=...  58.1 us
    reduce_scatter x1, waiting for transfers between devices, body(): lax.psum_scatter(product(hidden, down_mat), 'tensor', scatter_dimension=0...  51.7 us
    psum x2, blocking collectives, body(): summed = lax.psum(summed, over)  49.2 us
    dot_general x6, matrix products, product(): return jnp.dot(left, right, preferred_element_type=jnp.float32)  37.6 us
  transfers between devices with their start and end apart: 16, of which 13 were waited for; matrix products, arithmetic and copies ran while one was open for 7% of the time, Pallas kernels for 0%

profile of v1, /device:TPU:0, one launch (start us, length us, event | category | flops | bytes accessed | tf_op | source)
XLA Modules:
  0.0 1125.9 jit_solution(8896784130334329919)
XLA Ops:
  12.3 32.9 %all_gather.34 = bf16[192,768]{0,1:T(8,128)(2,1)S(1)} all-gather(bf16[192,96]{0,1:T(8,128)(2,1)S(1)} %copy.49), channel_id=1, replica_groups=mesh['dp'=8,'tensor'=4] {'dp'}, dimensions={1}, use_global_device_ids=true | all-gather | bytes 331776 | tf_op jit(solution)/shard_map/all_gather | solution.py:148
  45.2 31.3 %all_gather.31 = bf16[768,192]{1,0:T(8,128)(2,1)S(1)} all-gather(bf16[96,192]{1,0:T(8,128)(2,1)} %param.26), channel_id=1, replica_groups=mesh['dp'=8,'tensor'=4] {'dp'}, dimensions={0}, use_global_device_ids=true | all-gather | bytes 331776 | tf_op jit(solution)/shard_map/all_gather | solution.py:145
  76.6 31.5 %all_gather.32 = bf16[768,192]{1,0:T(8,128)(2,1)S(1)} all-gather(bf16[96,192]{1,0:T(8,128)(2,1)} %param.27), channel_id=1, replica_groups=mesh['dp'=8,'tensor'=4] {'dp'}, dimensions={0}, use_global_device_ids=true | all-gather | bytes 331776 | tf_op jit(solution)/shard_map/all_gather | solution.py:146
  108.1 33.2 %all_gather.33 = bf16[768,192]{1,0:T(8,128)(2,1)} all-gather(bf16[96,192]{1,0:T(8,128)(2,1)} %param.28), channel_id=1, replica_groups=mesh['dp'=8,'tensor'=4] {'dp'}, dimensions={0}, use_global_device_ids=true | all-gather | bytes 331776 | tf_op jit(solution)/shard_map/all_gather | solution.py:147
  143.2 3.1 fusion.43
  147.3 3.2 convolution_convert_fusion.1
  151.8 36.4 %while.27 = (s32[]{:T(128)}, bf16[4,512,3,64]{1,3,2,0:T(8,128)(2,1)S(1)}, f32[4,3,512]{2,1,0:T(4,128)}, pred[2048]{0:T(1024)(128)(4,1)S(1)}, bf16[4,512,3,64]{1,...) while((s32[]{:T(128)}, ...), condition=%wide.region_3.4_spmd, body=%wide.region_0.3_spmd.sunk | while | flops 843053568 | bytes 39972968 | solution.py:61
  153.8 2.8 fusion.131
  156.6 3.7 fusion.132
  162.9 2.8 fusion.131
  165.7 3.7 fusion.132
  172.0 2.8 fusion.131
  174.8 3.7 fusion.132
  181.1 2.8 fusion.131
  183.9 3.7 fusion.132
  189.9 3.7 fusion.60
  195.0 58.1 %reduce-scatter.19.cloned.1.call-done = f32[512,768]{1,0:T(8,128)} async-done(((f32[2048,768]{1,0:T(8,128)}), f32[512,768]{1,0:T(8,128)}) %reduce-scatter.19.cloned.1.call-update) | async-done | bytes 1572880 | tf_op jit(solution)/shard_map/reduce_scatter | solution.py:170
  259.2 26.4 %all-gather.9.cloned.1.call-done = bf16[2048,768]{1,0:T(8,128)(2,1)} async-done(((bf16[512,768]{1,0:T(8,128)(2,1)}), bf16[2048,768]{1,0:T(8,128)(2,1)}) %all-gather.9.cloned.1.call-update) | async-done | bytes 3145744 | tf_op jit(solution)/shard_map/all_gather | solution.py:180
  285.6 18.9 %multiply_convert_fusion.1 = (bf16[2048,768]{1,0:T(8,128)(2,1)}, f32[2048,768]{1,0:T(8,128)}, f32[2048,768]{1,0:T(8,128)}) fusion(f32[768]{0:T(1024)} %convert_element_type.139, bf16[2048,768]{1,0:T(8,128)(2,1)} %all-gather.9.cloned.1.call-done, bf16[768,768]{1,0:T(8,128)(2,1)} %all-gather.11.cloned.1.call-done), kind=kOutput, calls=%fused_computation.47 | convolution fusion | flops 2519728128 | bytes 20057088 | tf_op jit(solution)/shard_map/dot_general | solution.py:24
  304.5 24.9 %all-gather.13.cloned.1.call-done = bf16[768,768]{0,1:T(8,128)(2,1)} async-done(((bf16[768,96]{0,1:T(8,128)(2,1)}), bf16[768,768]{0,1:T(8,128)(2,1)}) %all-gather.13.cloned.1.call-update) | async-done | bytes 1179664 | tf_op jit(solution)/shard_map/all_gather | solution.py:150
  329.4 7.5 fusion.61
  342.1 51.7 %reduce-scatter.21.cloned.1.call-done = f32[512,768]{1,0:T(8,128)} async-done(((f32[2048,768]{1,0:T(8,128)}), f32[512,768]{1,0:T(8,128)}) %reduce-scatter.21.cloned.1.call-update) | async-done | bytes 1572880 | tf_op jit(solution)/shard_map/reduce_scatter | solution.py:184
  393.8 4.2 fusion.49
  404.5 28.2 %all-gather.15.cloned.1.call-done = bf16[2048,768]{1,0:T(8,128)(2,1)} async-done(((bf16[512,768]{1,0:T(8,128)(2,1)}), bf16[2048,768]{1,0:T(8,128)(2,1)}) %all-gather.15.cloned.1.call-update) | async-done | bytes 3145744 | tf_op jit(solution)/shard_map/all_gather | solution.py:194
  432.7 11.1 convert_reduce_fusion
  445.4 4.6 fusion.62
  450.1 58.3 %reduce-scatter.23.cloned.1.call-done = f32[512,768]{1,0:T(8,128)} async-done(((f32[2048,768]{1,0:T(8,128)}), f32[512,768]{1,0:T(8,128)}) %reduce-scatter.23.cloned.1.call-update) | async-done | bytes 1572880 | tf_op jit(solution)/shard_map/reduce_scatter | solution.py:203
  508.4 3.3 multiply_reduce_fusion.1
  516.1 28.4 %all-gather.17.cloned.1.call-done = bf16[2048,768]{1,0:T(8,128)(2,1)} async-done(((bf16[512,768]{1,0:T(8,128)(2,1)}), bf16[2048,768]{1,0:T(8,128)(2,1)}) %all-gather.17.cloned.1.call-update) | async-done | bytes 3145744 | tf_op jit(solution)/shard_map/all_gather | solution.py:209
  544.6 4.0 convolution_convert_fusion
  549.5 119.3 %while.28 = (s32[]{:T(128)}, f32[2048,3,64]{0,2,1:T(8,128)S(1)}, f32[2048,3,64]{0,2,1:T(8,128)}, bf16[4,512,3,64]{1,3,2,0:T(8,128)(2,1)}, s32[4]{0:T(128)S(1)}, ...) while((s32[]{:T(128)}, f32[2048,3,64]{0,2,1:T(8,128)S(1)}, ...), condition=%wide.region_17.18_spmd.clone, body=%wide.region_15.17_spmd.clone.sunk | while | flops 2062514688 | bytes 129417528 | solution.py:103
  553.4 2.8 fusion.142
  556.1 4.9 fusion.144
  561.0 4.8 multiply_reduce_fusion.6
  565.9 5.0 multiply_convert_fusion.3
  570.9 5.6 fusion.145
  582.8 2.8 fusion.142
  585.5 5.5 fusion.144
  591.0 4.8 multiply_reduce_fusion.6
  595.9 5.0 multiply_convert_fusion.3
  600.9 5.6 fusion.145
  612.7 2.8 fusion.142
  615.5 5.5 fusion.144
  621.0 4.8 multiply_reduce_fusion.6
  625.9 5.0 multiply_convert_fusion.3
  630.8 5.6 fusion.145
  645.5 5.5 fusion.144
  651.0 4.8 multiply_reduce_fusion.6
  655.9 5.0 multiply_convert_fusion.3
  660.8 5.6 fusion.145
  668.9 4.5 convolution_bitcast_fusion
  678.3 2.8 add_convert_fusion
  681.2 7.0 fusion.65
  688.2 6.9 fusion.66
  695.2 3.5 convolution_bitcast_fusion.3
  705.4 3.7 convolution_bitcast_fusion.1
  715.7 10.8 all-reduce.1
  726.5 38.4 %all-reduce = (f32[768]{0:T(1024)S(1)}, f32[768]{0:T(1024)S(1)}, f32[768]{0:T(1024)}, f32[3072]{0:T(1024)S(1)}, f32[768]{0:T(1024)}, /*index=5*/f32[768]{0:T(102...) all-reduce(f32[768]{0:T(1024)S(1)} %get-tuple-element.286, ...), channel_id=1, replica_groups=mesh['dp'=8,'tensor'=4] {'dp'}, use_global_device_ids=true, to_apply=%region_27.28 | all-reduce | flops 9219 | bytes 73752 | tf_op jit(solution)/shard_map/psum | solution.py:266
  769.0 6.5 reduce-scatter.25.cloned.1.call-done
  777.8 71.1 %reduce-scatter.27.cloned.1.call-done = f32[96,768]{1,0:T(8,128)} async-done(((f32[768,768]{1,0:T(8,128)}), f32[96,768]{1,0:T(8,128)}) %reduce-scatter.27.cloned.1.call-update) | async-done | bytes 294928 | tf_op jit(solution)/shard_map/reduce_scatter | solution.py:230
  848.8 72.4 %reduce-scatter.29.cloned.1.call-done = f32[768,96]{0,1:T(8,128)} async-done(((f32[768,768]{0,1:T(8,128)}), f32[768,96]{0,1:T(8,128)}) %reduce-scatter.29.cloned.1.call-update) | async-done | bytes 294928 | tf_op jit(solution)/shard_map/reduce_scatter | solution.py:231
  921.2 65.9 %reduce-scatter.31.cloned.1.call-done = f32[96,192]{1,0:T(8,128)} async-done(((f32[768,192]{1,0:T(8,128)}), f32[96,192]{1,0:T(8,128)}) %reduce-scatter.31.cloned.1.call-update) | async-done | bytes 73744
  987.1 65.4 %reduce-scatter.33.cloned.1.call-done = f32[96,192]{1,0:T(8,128)} async-done(((f32[768,192]{1,0:T(8,128)}), f32[96,192]{1,0:T(8,128)}) %reduce-scatter.33.cloned.1.call-update) | async-done | bytes 73744
  1052.5 65.8 %reduce-scatter.35.cloned.1.call-done = f32[96,192]{1,0:T(8,128)} async-done(((f32[768,192]{1,0:T(8,128)}), f32[96,192]{1,0:T(8,128)}) %reduce-scatter.35.cloned.1.call-update) | async-done | bytes 73744
  (202 shorter events, 87.7 us)
Async XLA Ops:
  8.0 135.2 %all-gather.7.cloned.1.call-start = ((), (), s32[]{:S(2)}) async-start(), calls=%async_computation.10 | async-start | bytes 3932160 | tf_op jit(solution)/shard_map/all_gather | solution.py:157
  8.8 244.3 %reduce-scatter.19.cloned.1.call-start = ((), (), s32[]{:S(2)}) async-start(), calls=%async_computation.11 | async-start | bytes 7864320 | tf_op jit(solution)/shard_map/reduce_scatter | solution.py:170
  76.6 70.3 %copy-start.11 = (bf16[768,192]{1,0:T(8,128)(2,1)}, bf16[768,192]{1,0:T(8,128)(2,1)S(1)}, u32[]{:S(2)}) copy-start(bf16[768,192]{1,0:T(8,128)(2,1)S(1)} %all_gather.31) | copy-start | bytes 884740
  108.0 39.3 %copy-start.8 = (bf16[768,192]{1,0:T(8,128)(2,1)}, bf16[768,192]{1,0:T(8,128)(2,1)S(1)}, u32[]{:S(2)}) copy-start(bf16[768,192]{1,0:T(8,128)(2,1)S(1)} %all_gather.32) | copy-start | bytes 884740
  146.2 0.9 copy-start.5
  147.1 3.4 copy-start.1
  147.1 3.4 copy-start.13
  189.0 0.9 copy-start.7
  193.7 0.7 copy-start.30
  193.7 0.7 copy-start.31
  193.7 0.7 copy-start.32
  193.7 65.5 %all-gather.11.cloned.1.call-start = ((), (), s32[]{:S(2)}) async-start(), calls=%async_computation.13 | async-start | bytes 1327104 | tf_op jit(solution)/shard_map/all_gather | solution.py:149
  194.3 91.3 %all-gather.9.cloned.1.call-start = ((), (), s32[]{:S(2)}) async-start(), calls=%async_computation.12 | async-start | bytes 3932160 | tf_op jit(solution)/shard_map/all_gather | solution.py:180
  194.4 60.6 %copy-start.17 = (f32[768]{0:T(1024)}, f32[768]{0:T(1024)S(1)}, u32[]{:S(2)}) copy-start(f32[768]{0:T(1024)S(1)} %convert_element_type.135) | copy-start | bytes 9220
  253.1 2.8 copy-start.15
  255.3 0.6 copy-start.18
  257.1 72.4 %all-gather.13.cloned.1.call-start = ((), (), s32[]{:S(2)}) async-start(), calls=%async_computation.14 | async-start | bytes 1327104 | tf_op jit(solution)/shard_map/all_gather | solution.py:150
  257.7 136.1 %reduce-scatter.21.cloned.1.call-start = ((), (), s32[]{:S(2)}) async-start(), calls=%async_computation.15 | async-start | bytes 7864320 | tf_op jit(solution)/shard_map/reduce_scatter | solution.py:184
  337.0 95.7 %all-gather.15.cloned.1.call-start = ((), (), s32[]{:S(2)}) async-start(), calls=%async_computation.16 | async-start | bytes 3932160 | tf_op jit(solution)/shard_map/all_gather | solution.py:194
  393.8 4.5 copy-start.10
  393.8 4.5 copy-start.16
  398.0 1.6 copy-start.26
  401.1 1.2 copy-start.4
  401.1 2.8 copy-start.19
  404.0 104.4 %reduce-scatter.23.cloned.1.call-start = ((), (), s32[]{:S(2)}) async-start(), calls=%async_computation.17 | async-start | bytes 7864320 | tf_op jit(solution)/shard_map/reduce_scatter | solution.py:203
  432.7 12.7 %copy-start.33 = (bf16[768,768]{1,0:T(8,128)(2,1)S(1)}, bf16[768,768]{1,0:T(8,128)(2,1)}, u32[]{:S(2)}) copy-start(bf16[768,768]{1,0:T(8,128)(2,1)} %all-gather.11.cloned.1.call-done) | copy-start | bytes 3538948
  443.8 1.7 copy-start.35
  450.0 94.5 %all-gather.17.cloned.1.call-start = ((), (), s32[]{:S(2)}) async-start(), calls=%async_computation.18 | async-start | bytes 3932160 | tf_op jit(solution)/shard_map/all_gather | solution.py:209
  513.0 1.2 copy-start.2
  513.0 2.8 copy-start.20
  515.9 251.5 %reduce-scatter.37.cloned.1.call-start = ((), (), s32[]{:S(2)}) async-start(), calls=%async_computation.25 | async-start | bytes 884736
  570.9 5.6 copy-start
  600.8 5.6 copy-start
  630.8 5.6 copy-start
  660.8 5.6 copy-start
  668.9 4.8 copy-start.9
  673.4 102.1 %reduce-scatter.25.cloned.1.call-start = ((), (), s32[]{:S(2)}) async-start(), calls=%async_computation.19 | async-start | bytes 3932160 | tf_op jit(solution)/shard_map/reduce_scatter | solution.py:221
  673.7 2.7 copy-start.6
  674.8 2.5 copy-start.12
  677.2 1.1 copy-start.14
  681.1 167.7 %reduce-scatter.27.cloned.1.call-start = ((), (), s32[]{:S(2)}) async-start(), calls=%async_computation.20 | async-start | bytes 2654208 | tf_op jit(solution)/shard_map/reduce_scatter | solution.py:230
  688.2 233.0 %reduce-scatter.29.cloned.1.call-start = ((), (), s32[]{:S(2)}) async-start(), calls=%async_computation.21 | async-start | bytes 2654208 | tf_op jit(solution)/shard_map/reduce_scatter | solution.py:231
  695.2 291.9 %reduce-scatter.31.cloned.1.call-start = ((), (), s32[]{:S(2)}) async-start(), calls=%async_computation.22 | async-start | bytes 884736
  701.0 351.5 %reduce-scatter.33.cloned.1.call-start = ((), (), s32[]{:S(2)}) async-start(), calls=%async_computation.23 | async-start | bytes 884736
  705.0 6.3 copy-start.34
  705.0 9.6 copy-start.29
  705.0 10.7 copy-start.22
  705.0 10.6 copy-start.23
  705.0 10.6 copy-start.24
  705.0 10.6 copy-start.25
  705.0 10.6 copy-start.27
  705.0 10.6 copy-start.28
  705.1 70.4 %copy-start.3 = (f32[512,768]{1,0:T(8,128)S(1)}, f32[512,768]{1,0:T(8,128)}, u32[]{:S(2)}) copy-start(f32[512,768]{1,0:T(8,128)} %copy-done.2) | copy-start | bytes 4718596
  705.1 70.4 %copy-start.21 = (f32[512]{0:T(512)S(1)}, f32[512]{0:T(512)}, u32[]{:S(2)}) copy-start(f32[512]{0:T(512)} %copy-done.20) | copy-start | bytes 6148
  705.1 413.3 %reduce-scatter.35.cloned.1.call-start = ((), (), s32[]{:S(2)}) async-start(), calls=%async_computation.24 | async-start | bytes 884736
Sparse Core Ops, SparseCore 0:
  10.4 31.2 all-gather.6
  193.8 59.2 reduce-scatter.18
  404.1 28.5 all-gather.14
  516.0 28.5 all-gather.16
Sparse Core Ops, SparseCore 1:
  196.6 42.3 all-gather.10
  257.2 28.4 all-gather.8
  287.9 41.5 all-gather.12
  337.0 56.7 reduce-scatter.20
  450.1 58.2 reduce-scatter.22
  673.5 62.5 reduce-scatter.36
  738.5 36.9 reduce-scatter.24
  779.8 68.9 reduce-scatter.26
  853.2 68.0 reduce-scatter.28
  925.4 61.6 reduce-scatter.30
  990.9 61.6 reduce-scatter.32
  1056.7 61.5 reduce-scatter.34
